TPU v7x, 32 devices: a whole 2x2x4 slice. The times are simulated.
32 devices in a mesh: groups: 2 (over y), sect: 4 (over x, core), hid: 4 (over z).
Axes of the slice: x: 2, y: 2, z: 4, core: 2. Of those that a mesh axis runs over, the one named last changes fastest.
Arguments:
- resid: bfloat16 [1024, 4096], P(('groups', 'sect'), 'hid'), parts along dimension 0, may hold values from -64 to 64
- moe_gain: bfloat16 [4096], replicated, may hold values from 0.25 to 1.75
- routes: int32 [1024, 2], P(('groups', 'sect')), parts along dimension 0, may hold values from 0 to 3, all different within a row; in each aligned block of 128 rows (0 to 127, 128 to 255, ...) at most 128 rows name the same one
- gate_q: int32 [1024, 2], P(('groups', 'sect')), parts along dimension 0, may hold values from 16 to 255
- doc_lengths: int32 [8, 4], P(('groups', 'sect')), parts along dimension 0, may hold values from 1 to 64, 128 in all within a row
- w_gate: bfloat16 [4, 4096, 4096], P('sect', None, 'hid'), may hold values from -0.09375 to 0.09375
- w_up: bfloat16 [4, 4096, 4096], P('sect', None, 'hid'), may hold values from -0.09375 to 0.09375
- w_down: bfloat16 [4, 4096, 4096], P('sect', 'hid'), may hold values from -0.09375 to 0.09375
- attn_gain: bfloat16 [4096], replicated, may hold values from 0.25 to 1.75
- w_q: bfloat16 [4096, 4096], P('sect', 'hid')
- w_k: bfloat16 [4096, 1024], P('sect', 'hid')
- w_v: bfloat16 [4096, 1024], P('sect', 'hid'), may hold values from -0.09375 to 0.09375
Outputs:
- new_resid: bfloat16 [1024, 4096], P(('groups', 'sect'), 'hid'), parts along dimension 0
- context: bfloat16 [1024, 4096], P(('groups', 'sect'), 'hid'), parts along dimension 0
There are 2 independent parts, one for each index of `groups`. A program takes and returns all parts, laid end to end along the dimension named above; an argument that names none is the same for every part. Nothing has to cross between parts.
Inputs may be any that keep to these rules, and one draw needn't show every extreme that they name: `routes`: within the rows of one index of sect (aligned blocks of 128 rows) no expert is named by more than 128 rows. `doc_lengths`: each row sums to 128.
All inputs are finite; a program needn't handle non-finite values.
Results may differ from a plain program's by a relative error of at most 0.012.
The roundings to bfloat16 on the way count: a program that leaves them out, or rounds other values in their place, can miss the bound.
Values may be sent and summed in bfloat16 or wider, within the bound.
No kernel may reach another device: no remote copies, remote signals or barrier semaphores. Data moves between devices by JAX's collectives and lax.ppermute only.
A program may use at most 128 MiB of HBM per device.

v0:
```python
import math
import jax
import jax.numpy as jnp
from jax import lax
from jax.sharding import PartitionSpec as P

H = 32
KVH = 8
HD = 128


def layer_norm(values, gain):
    center = values - jnp.mean(values, axis=1, keepdims=True)
    spread = jnp.mean(center * center, axis=1, keepdims=True)
    return (center * lax.rsqrt(spread + 1e-05) * gain.astype(jnp.float32)).astype(jnp.bfloat16)


def slot_targets(route_rows, experts, capacity):
    flat = route_rows.reshape(-1)
    onehot = (flat[:, None] == jnp.arange(experts, dtype=jnp.int32)[None, :]).astype(jnp.int32)
    before = jnp.cumsum(onehot, axis=0, dtype=jnp.int32) - onehot
    return flat * capacity + jnp.sum(before * onehot, axis=1, dtype=jnp.int32)


def source_rows(targets, experts, capacity):
    count = targets.shape[0]
    filler = jnp.full((experts * capacity,), count, jnp.int32)
    return filler.at[targets].set(jnp.arange(count, dtype=jnp.int32)) // 2


def rotate(values, position, head):
    count = values.shape[0]
    split_heads = values.reshape(count, -1, head)
    half = head // 2
    freqs = jnp.exp(jnp.arange(half, dtype=jnp.float32) * (-2.0 * math.log(10000.0) / head))
    angles = position[:, None, None] * freqs[None, None, :]
    cosine = jnp.cos(angles)
    sine = jnp.sin(angles)
    first = split_heads[:, :, :half]
    second = split_heads[:, :, half:]
    turned = jnp.concatenate(
        [first * cosine - second * sine, second * cosine + first * sine], axis=2
    )
    return turned.reshape(count, -1)


def attend(query, keys, vals, lengths, head, group):
    count = query.shape[0]
    kv_heads = keys.shape[1] // head
    ends = jnp.cumsum(lengths, dtype=jnp.int32)
    places = jnp.arange(count, dtype=jnp.int32)
    after = (places[:, None] >= ends[None, :]).astype(jnp.int32)
    doc_ids = jnp.sum(after, axis=1, dtype=jnp.int32)
    starts = jnp.sum(after * lengths[None, :], axis=1, dtype=jnp.int32)
    position = (places - starts).astype(jnp.float32)
    rotated_q = (
        rotate(query, position, head).astype(jnp.bfloat16).reshape(count, kv_heads, group, head)
    )
    rotated_k = rotate(keys, position, head).astype(jnp.bfloat16).reshape(count, kv_heads, head)
    value_heads = vals.reshape(count, kv_heads, head)
    allowed = (doc_ids[:, None] == doc_ids[None, :]) & (places[None, :] <= places[:, None])
    scores = jnp.einsum(
        "tkgd,skd->kgts", rotated_q, rotated_k, preferred_element_type=jnp.float32
    ) * (1.0 / math.sqrt(head))
    scores = jnp.where(allowed[None, None], scores, -jnp.inf)
    highest = jnp.max(scores, axis=3, keepdims=True)
    weights = jnp.exp(scores - highest)
    probs = (weights / jnp.sum(weights, axis=3, keepdims=True)).astype(jnp.bfloat16)
    mixed = jnp.einsum("kgts,skd->tkgd", probs, value_heads, preferred_element_type=jnp.float32)
    return mixed.astype(jnp.bfloat16).reshape(count, -1)


def on_device(
    resid, moe_gain, routes, gate_q, doc_lengths, w_gate, w_up, w_down, attn_gain, w_q, w_k, w_v
):
    sections = lax.axis_size("sect")
    slices = lax.axis_size("hid")
    tokens_here, local_width = resid.shape
    width = local_width * slices
    capacity = 4 * tokens_here // sections
    entry = lax.all_gather(resid, "hid", axis=1, tiled=True)
    normed = layer_norm(entry.astype(jnp.float32), moe_gain)
    targets = slot_targets(routes, sections, capacity)
    sources = source_rows(targets, sections, capacity)
    padded = jnp.concatenate([normed, jnp.zeros((1, width), jnp.bfloat16)], axis=0)
    gate_w = w_gate[0]
    up_w = w_up[0]
    down_w = w_down[0]
    outgoing = padded[sources].reshape(sections, capacity, width)
    arrived = lax.all_to_all(outgoing, "sect", split_axis=0, concat_axis=0, tiled=True).reshape(
        sections * capacity, width
    )
    gate = jnp.dot(arrived, gate_w, preferred_element_type=jnp.float32)
    up = jnp.dot(arrived, up_w, preferred_element_type=jnp.float32)
    hidden = (jax.nn.silu(gate) * up).astype(jnp.bfloat16)
    weights = gate_q.reshape(-1).astype(jnp.float32) / 256.0
    own_resid = resid.astype(jnp.float32)
    outputs = jnp.dot(hidden, down_w, preferred_element_type=jnp.float32)
    mine = lax.psum_scatter(outputs, "hid", scatter_dimension=1, tiled=True)
    returned = lax.all_to_all(
        mine.reshape(sections, capacity, local_width),
        "sect",
        split_axis=0,
        concat_axis=0,
        tiled=True,
    )
    picked = returned.reshape(sections * capacity, local_width)[targets]
    mixture = jnp.sum((picked * weights[:, None]).reshape(tokens_here, 2, local_width), axis=1)
    new_local = (own_resid + mixture).astype(jnp.bfloat16)
    full_rows = lax.all_gather(new_local, "hid", axis=1, tiled=True)
    normed_next = layer_norm(full_rows.astype(jnp.float32), attn_gain)
    query = jnp.dot(
        normed_next,
        lax.all_gather(w_q, "sect", axis=0, tiled=True),
        preferred_element_type=jnp.float32,
    )
    keys = jnp.dot(
        normed_next,
        lax.all_gather(w_k, "sect", axis=0, tiled=True),
        preferred_element_type=jnp.float32,
    )
    vals = jnp.dot(
        normed_next,
        lax.all_gather(w_v, "sect", axis=0, tiled=True),
        preferred_element_type=jnp.float32,
    )
    context = attend(query, keys, vals.astype(jnp.bfloat16), doc_lengths[0], HD, H // KVH)
    return (new_local, context)


def solution(mesh):
    in_specs = (
        P(("groups", "sect"), "hid"),
        P(),
        P(("groups", "sect"), None),
        P(("groups", "sect"), None),
        P(("groups", "sect"), None),
        P("sect", None, "hid"),
        P("sect", None, "hid"),
        P("sect", "hid", None),
        P(),
        P("sect", "hid"),
        P("sect", "hid"),
        P("sect", "hid"),
    )
    out_specs = (P(("groups", "sect"), "hid"), P(("groups", "sect"), "hid"))
    return jax.shard_map(
        on_device, mesh=mesh, in_specs=in_specs, out_specs=out_specs, check_vma=False
    )
```

profile of v0, /device:TPU:0, one launch (start us, length us, event | category | flops | bytes accessed | tf_op | source)
XLA Modules:
  0.0 450.2 jit_solution(11100007344031387848)
XLA Ops:
  9.7 1.2 reduce-window.18
  12.3 1.4 scatter_custom_fusion
  13.7 26.5 %all-gather.6.cloned.1.call-done = bf16[128,4096]{1,0:T(8,128)(2,1)} async-done(((bf16[128,1024]{1,0:T(8,128)(2,1)}), bf16[128,4096]{1,0:T(8,128)(2,1)}) %all-gather.6.cloned.1.call-update) | async-done | bytes 1048592 | tf_op jit(solution)/shard_map/all_gather | solution.py:81
  40.2 1.5 convert_reduce_fusion.1
  41.8 1.7 fusion.14
  44.0 4.4 gather_fusion
  48.3 51.9 %all_to_all.10 = bf16[4,128,4096]{2,1,0:T(8,128)(2,1)S(1)} all-to-all(bf16[4,128,4096]{2,1,0:T(8,128)(2,1)} %bitcast.87), channel_id=1, replica_groups=mesh['groups'=2,'sect'=4,'hid'=4] {'sect'}, dimensions={0} | all-to-all | bytes 8388608 | tf_op jit(solution)/shard_map/all_to_all | solution.py:90
  100.2 2.0 copy-done.1
  102.2 6.9 %fusion.5 = f32[512,1024]{1,0:T(8,128)S(1)} fusion(bf16[512,4096]{1,0:T(8,128)(2,1)S(1)} %bitcast.89, bf16[1,4096,1024]{2,1,0:T(8,128)(2,1)} %param.17), kind=kOutput, calls=%fused_computation.8 | convolution fusion | flops 4294967296 | bytes 14680064 | tf_op jit(solution)/shard_map/dot_general | solution.py:93
  109.1 19.1 %fusion.1 = f32[512,4096]{1,0:T(8,128)} fusion(bf16[1,1024,4096]{2,1,0:T(8,128)(2,1)} %param.19, f32[512,1024]{1,0:T(8,128)S(1)} %fusion.5, bf16[512,4096]{1,0:T(8,128)(2,1)} %bitcast.90, bf16[1,4096,1024]{2,1,0:T(8,128)(2,1)} %param.18), kind=kOutput, calls=%fused_computation.4 | convolution fusion | flops 8593080320 | bytes 31457280 | tf_op jit(solution)/shard_map/dot_general | solution.py:98
  128.2 143.2 %reduce-scatter.2.cloned.1.call-done = f32[512,1024]{1,0:T(8,128)} async-done(((f32[512,4096]{1,0:T(8,128)}), f32[512,1024]{1,0:T(8,128)}) %reduce-scatter.2.cloned.1.call-update) | async-done | bytes 2097168 | tf_op jit(solution)/shard_map/reduce_scatter | solution.py:99
  271.4 3.7 all-to-all-start.1
  275.5 25.3 %all-to-all-done.1 = f32[4,128,1024]{2,1,0:T(8,128)S(1)} async-done(((f32[4,128,1024]{2,1,0:T(8,128)}), f32[4,128,1024]{2,1,0:T(8,128)S(1)}, u32[]{:S(2)}, u32[]{:S(2)}) %all-to-all-start.1) | async-done | bytes 2097184 | tf_op jit(solution)/shard_map/all_to_all | solution.py:100
  300.8 1.1 gather_fusion.1
  302.6 1.3 multiply_reduce_fusion
  307.2 25.4 %all-gather.8.cloned.1.call-done = bf16[128,4096]{1,0:T(8,128)(2,1)} async-done(((bf16[128,1024]{1,0:T(8,128)(2,1)}), bf16[128,4096]{1,0:T(8,128)(2,1)}) %all-gather.8.cloned.1.call-update) | async-done | bytes 1048592 | tf_op jit(solution)/shard_map/all_gather | solution.py:110
  332.6 1.5 convert_reduce_fusion
  334.2 1.7 fusion.11
  335.9 20.3 %all-gather.12.cloned.1.call-done = bf16[4096,256]{1,0:T(8,128)(2,1)} async-done(((bf16[1024,256]{1,0:T(8,128)(2,1)}), bf16[4096,256]{1,0:T(8,128)(2,1)}) %all-gather.12.cloned.1.call-update) | async-done | bytes 2097168 | tf_op jit(solution)/shard_map/all_gather | solution.py:119
  356.2 2.1 fusion.40
  358.4 57.5 %all-gather.14.cloned.1.call-done = bf16[4096,1024]{1,0:T(8,128)(2,1)} async-done(((bf16[1024,1024]{1,0:T(8,128)(2,1)}), bf16[4096,1024]{1,0:T(8,128)(2,1)}) %all-gather.14.cloned.1.call-update) | async-done | bytes 8388624 | tf_op jit(solution)/shard_map/all_gather | solution.py:114
  415.9 4.7 %convolution_bitcast_fusion = f32[16,8,8,128]{3,1,2,0:T(8,128)S(1)} fusion(bf16[4096,1024]{1,0:T(8,128)(2,1)} %all-gather.14.cloned.1.call-done, bf16[128,4096]{1,0:T(8,128)(2,1)S(1)} %copy-done.2, f32[4096]{0:T(1024)S(1)} %convert_element_type.80, f32[128]{0:T(128)S(1)} %add_rsqrt_fusion, f32[128]{0:T(128)S(1)} %broadcast_multiply_fusion.1), kind=kOutput, calls=%fused_computation.27 | convolution fusion | flops 1076363264 | bytes 9978880 | tf_op jit(solution)/shard_map/dot_general | solution.py:112
  422.1 17.9 %all-gather.10.cloned.1.call-done = bf16[4096,256]{1,0:T(8,128)(2,1)} async-done(((bf16[1024,256]{1,0:T(8,128)(2,1)}), bf16[4096,256]{1,0:T(8,128)(2,1)}) %all-gather.10.cloned.1.call-update) | async-done | bytes 2097168 | tf_op jit(solution)/shard_map/all_gather | solution.py:124
  439.9 2.1 convolution_convert_fusion.1
  (74 shorter events, 11.4 us)
Async XLA Ops:
  7.2 33.1 %all-gather.6.cloned.1.call-start = ((), (), s32[]{:S(2)}) async-start(), calls=%async_computation.3 | async-start | bytes 1310720 | tf_op jit(solution)/shard_map/all_gather | solution.py:81
  7.9 263.5 %reduce-scatter.2.cloned.1.call-start = ((), (), s32[]{:S(2)}) async-start(), calls=%async_computation.4 | async-start | bytes 10485760 | tf_op jit(solution)/shard_map/reduce_scatter | solution.py:99
  40.2 3.2 copy-start
  100.2 2.0 copy-start.1
  271.4 4.0 copy-start.5
  271.4 29.4 %all-to-all-start.1 = ((f32[4,128,1024]{2,1,0:T(8,128)}), f32[4,128,1024]{2,1,0:T(8,128)S(1)}, u32[]{:S(2)}, u32[]{:S(2)}) async-start(f32[4,128,1024]{2,1,0:T(8,128)} %bitcast.91), calls=%async_computation.2 | async-start | bytes 4194304 | tf_op jit(solution)/shard_map/all_to_all | solution.py:100
  275.2 57.5 %all-gather.8.cloned.1.call-start = ((), (), s32[]{:S(2)}) async-start(), calls=%async_computation.5 | async-start | bytes 1310720 | tf_op jit(solution)/shard_map/all_gather | solution.py:110
  301.9 2.0 copy-start.3
  303.9 2.6 copy-start.4
  303.9 2.6 copy-start.6
  304.7 51.4 %all-gather.12.cloned.1.call-start = ((), (), s32[]{:S(2)}) async-start(), calls=%async_computation.7 | async-start | bytes 2621440 | tf_op jit(solution)/shard_map/all_gather | solution.py:119
  305.3 110.6 %all-gather.14.cloned.1.call-start = ((), (), s32[]{:S(2)}) async-start(), calls=%async_computation.8 | async-start | bytes 10485760 | tf_op jit(solution)/shard_map/all_gather | solution.py:114
  305.9 134.0 %all-gather.10.cloned.1.call-start = ((), (), s32[]{:S(2)}) async-start(), calls=%async_computation.6 | async-start | bytes 2621440 | tf_op jit(solution)/shard_map/all_gather | solution.py:124
  332.6 23.5 %copy-start.2 = (bf16[128,4096]{1,0:T(8,128)(2,1)S(1)}, bf16[128,4096]{1,0:T(8,128)(2,1)}, u32[]{:S(2)}) copy-start(bf16[128,4096]{1,0:T(8,128)(2,1)} %all-gather.8.cloned.1.call-done) | copy-start | bytes 3145732
Sparse Core Ops, SparseCore 0:
  9.6 30.6 all-gather.5
  128.3 143.0 reduce-scatter.1
  304.9 27.7 all-gather.7
  334.1 22.0 all-gather.11
  357.6 58.2 all-gather.13
  417.3 22.5 all-gather.9
where the time goes:
time: 451 us; the launch traced here: 450 us
  waiting for transfers between devices  318 us (71%)
  blocking collectives  51.9 us (12%)
  matrix products  35.8 us (8%)
  between operations  14.4 us (3%)
  other arithmetic  12.8 us (3%)
  local copies, waits for them, and re-layouts  12.6 us (3%)
    reduce_scatter x1, waiting for transfers between devices, on_device(): mine = lax.psum_scatter(outputs, 'hid', scatter_dimension=1, tiled=True)  143 us
    all_gather x1, waiting for transfers between devices, on_device(): lax.all_gather(w_q, 'sect', axis=0, tiled=True)  57.5 us
    all_to_all x1, blocking collectives, on_device(): lax.all_to_all(outgoing, 'sect', split_axis=0, concat_axis=0, tiled=True)  51.9 us
    all_gather x1, waiting for transfers between devices, on_device(): entry = lax.all_gather(resid, 'hid', axis=1, tiled=True)  26.5 us
    all_gather x1, waiting for transfers between devices, on_device(): full_rows = lax.all_gather(new_local, 'hid', axis=1, tiled=True)  25.4 us
    all_to_all x1, waiting for transfers between devices, on_device(): lax.all_to_all(mine.reshape(sections, capacity, local_width), 'sect', spl...  25.3 us
    all_gather x1, waiting for transfers between devices, on_device(): lax.all_gather(w_k, 'sect', axis=0, tiled=True)  20.3 us
    dot_general x1, matrix products, on_device(): outputs = jnp.dot(hidden, down_w, preferred_element_type=jnp.float32)  19.1 us
  transfers between devices with their start and end apart: 7, of which 7 were waited for; matrix products, arithmetic and copies ran while one was open for 4% of the time, Pallas kernels for 0%

commit v1 on v0

--- a/solution.py
+++ b/solution.py
@@ -107,7 +107,12 @@
     picked = returned.reshape(sections * capacity, local_width)[targets]
     mixture = jnp.sum((picked * weights[:, None]).reshape(tokens_here, 2, local_width), axis=1)
     new_local = (own_resid + mixture).astype(jnp.bfloat16)
-    full_rows = lax.all_gather(new_local, "hid", axis=1, tiled=True)
+    ring = [new_local]
+    for hop in range(3):
+        ring.append(lax.ppermute(ring[-1], "hid", [(dev, (dev + 1) % 4) for dev in range(4)]))
+    full_rows = jnp.roll(
+        jnp.concatenate(ring[::-1], axis=1), (lax.axis_index("hid") + 1) * ring[0].shape[1], axis=1
+    )
     normed_next = layer_norm(full_rows.astype(jnp.float32), attn_gain)
     query = jnp.dot(
         normed_next,

time: 451 us -> 352 us (0.78)
  waiting for transfers between devices: 318 us -> 220 us
    all_gather x1, waiting for transfers between devices: 57.5 us -> 0.03 us  [on_device(): lax.all_gather(w_q, 'sect', axis=0, tiled=True)]
    all_gather x1 -> x0, waiting for transfers between devices: 25.4 us -> none  [on_device(): full_rows = lax.all_gather(new_local, 'hid', axis=1, tiled=True)]
    ppermute x0 -> x3, waiting for transfers between devices: none -> 24.6 us  [on_device(): lax.ppermute(ring[-1], 'hid', [(dev, (dev + 1) % 4) for dev in range(4)])]
    all_gather x1, waiting for transfers between devices: 20.3 us -> 0.03 us  [on_device(): lax.all_gather(w_k, 'sect', axis=0, tiled=True)]
    all_gather x1, waiting for transfers between devices: 17.9 us -> 0.03 us  [on_device(): lax.all_gather(w_v, 'sect', axis=0, tiled=True)]
  transfers between devices with their start and end apart: 7 -> 9, of which waited for: 7 -> 6; matrix products, arithmetic and copies ran while one was open for 4% -> 5% of each run, Pallas kernels for 0% -> 0%
where the time goes in v1:
time: 352 us
  waiting for transfers between devices  220 us (62%)
  blocking collectives  51.9 us (15%)
  matrix products  35.8 us (10%)
  between operations  16.1 us (5%)
  local copies, waits for them, and re-layouts  12.7 us (4%)
  other arithmetic  9.6 us (3%)
  starting transfers between devices  5.35 us (2%)
    reduce_scatter x1, waiting for transfers between devices, on_device(): mine = lax.psum_scatter(outputs, 'hid', scatter_dimension=1, tiled=True)  142 us
    all_to_all x1, blocking collectives, on_device(): lax.all_to_all(outgoing, 'sect', split_axis=0, concat_axis=0, tiled=True)  51.9 us
    all_gather x1, waiting for transfers between devices, on_device(): entry = lax.all_gather(resid, 'hid', axis=1, tiled=True)  26.5 us
    all_to_all x1, waiting for transfers between devices, on_device(): lax.all_to_all(mine.reshape(sections, capacity, local_width), 'sect', spl...  25.3 us
    ppermute x3, waiting for transfers between devices, on_device(): lax.ppermute(ring[-1], 'hid', [(dev, (dev + 1) % 4) for dev in range(4)])  24.6 us
    dot_general x1, matrix products, on_device(): outputs = jnp.dot(hidden, down_w, preferred_element_type=jnp.float32)  19.1 us
  transfers between devices with their start and end apart: 9, of which 6 were waited for; matrix products, arithmetic and copies ran while one was open for 5% of the time, Pallas kernels for 0%

profile of v1, /device:TPU:0, one launch (start us, length us, event | category | flops | bytes accessed | tf_op | source)
XLA Modules:
  0.0 351.8 jit_solution(8776761472502916845)
XLA Ops:
  8.8 0.8 copy.36
  10.6 1.2 reduce-window.18
  13.1 1.4 scatter_custom_fusion
  14.6 26.5 %all-gather.5.cloned.1.call-done = bf16[128,4096]{1,0:T(8,128)(2,1)} async-done(((bf16[128,1024]{1,0:T(8,128)(2,1)}), bf16[128,4096]{1,0:T(8,128)(2,1)}) %all-gather.5.cloned.1.call-update) | async-done | bytes 1048592 | tf_op jit(solution)/shard_map/all_gather | solution.py:81
  41.1 1.5 convert_reduce_fusion.1
  42.6 1.7 fusion.14
  44.8 4.4 %gather_fusion = bf16[512,4096]{1,0:T(8,128)(2,1)} fusion(bf16[129,4096]{1,0:T(8,128)(2,1)S(1)} %concatenate.17, s32[1024]{0:T(1024)S(1)} %pad_clamp_fusion.1), kind=kCustom, calls=%fused_computation | custom fusion | bytes 8390656 | tf_op jit(solution)/shard_map/gather | solution.py:89
  49.2 51.9 %all_to_all.10 = bf16[4,128,4096]{2,1,0:T(8,128)(2,1)S(1)} all-to-all(bf16[4,128,4096]{2,1,0:T(8,128)(2,1)} %bitcast.87), channel_id=1, replica_groups=mesh['groups'=2,'sect'=4,'hid'=4] {'sect'}, dimensions={0} | all-to-all | bytes 8388608 | tf_op jit(solution)/shard_map/all_to_all | solution.py:90
  101.1 1.9 copy-done.1
  103.0 6.9 %fusion.5 = f32[512,1024]{1,0:T(8,128)S(1)} fusion(bf16[512,4096]{1,0:T(8,128)(2,1)S(1)} %bitcast.89, bf16[1,4096,1024]{2,1,0:T(8,128)(2,1)} %param.17), kind=kOutput, calls=%fused_computation.8 | convolution fusion | flops 4294967296 | bytes 14680064 | tf_op jit(solution)/shard_map/dot_general | solution.py:93
  109.9 19.1 %fusion.1 = f32[512,4096]{1,0:T(8,128)} fusion(bf16[1,1024,4096]{2,1,0:T(8,128)(2,1)} %param.19, f32[512,1024]{1,0:T(8,128)S(1)} %fusion.5, bf16[512,4096]{1,0:T(8,128)(2,1)} %bitcast.90, bf16[1,4096,1024]{2,1,0:T(8,128)(2,1)} %param.18), kind=kOutput, calls=%fused_computation.4 | convolution fusion | flops 8593080320 | bytes 31457280 | tf_op jit(solution)/shard_map/dot_general | solution.py:98
  130.1 142.1 %reduce-scatter.2.cloned.1.call-done = f32[512,1024]{1,0:T(8,128)} async-done(((f32[512,4096]{1,0:T(8,128)}), f32[512,1024]{1,0:T(8,128)}) %reduce-scatter.2.cloned.1.call-update) | async-done | bytes 2097168 | tf_op jit(solution)/shard_map/reduce_scatter | solution.py:99
  272.2 3.7 %all-to-all-start.1 = ((f32[4,128,1024]{2,1,0:T(8,128)}), f32[4,128,1024]{2,1,0:T(8,128)S(1)}, u32[]{:S(2)}, u32[]{:S(2)}) async-start(f32[4,128,1024]{2,1,0:T(8,128)} %bitcast.91), calls=%async_computation.2 | async-start | bytes 4194304 | tf_op jit(solution)/shard_map/all_to_all | solution.py:100
  276.3 25.3 %all-to-all-done.1 = f32[4,128,1024]{2,1,0:T(8,128)S(1)} async-done(((f32[4,128,1024]{2,1,0:T(8,128)}), f32[4,128,1024]{2,1,0:T(8,128)S(1)}, u32[]{:S(2)}, u32[]{:S(2)}) %all-to-all-start.1) | async-done | bytes 2097184 | tf_op jit(solution)/shard_map/all_to_all | solution.py:100
  301.6 1.1 gather_fusion.1
  303.3 1.3 multiply_reduce_fusion
  304.8 1.2 collective-permute-start
  306.3 8.2 %collective-permute-done = bf16[128,1024]{1,0:T(8,128)(2,1)S(1)} collective-permute-done((bf16[128,1024]{1,0:T(8,128)(2,1)S(1)}, bf16[128,1024]{1,0:T(8,128)(2,1)S(1)}, u32[]{:S(2)}, u32[]{:S(2)}) %collective-permute-start) | collective-permute-done | bytes 262176 | tf_op jit(solution)/shard_map/ppermute | solution.py:112
  314.6 8.6 %collective-permute-done.1 = bf16[128,1024]{1,0:T(8,128)(2,1)S(1)} collective-permute-done((bf16[128,1024]{1,0:T(8,128)(2,1)S(1)}, bf16[128,1024]{1,0:T(8,128)(2,1)S(1)}, u32[]{:S(2)}, u32[]{:S(2)}) %collective-permute-start.1) | collective-permute-done | bytes 262176 | tf_op jit(solution)/shard_map/ppermute | solution.py:112
  323.6 7.8 %collective-permute-done.2 = bf16[128,1024]{1,0:T(8,128)(2,1)S(1)} collective-permute-done((bf16[128,1024]{1,0:T(8,128)(2,1)S(1)}, bf16[128,1024]{1,0:T(8,128)(2,1)S(1)}, u32[]{:S(2)}, u32[]{:S(2)}) %collective-permute-start.2) | collective-permute-done | bytes 262176 | tf_op jit(solution)/shard_map/ppermute | solution.py:112
  332.4 2.1 fusion.40
  334.6 4.7 %convolution_bitcast_fusion = f32[16,8,8,128]{3,1,2,0:T(8,128)S(1)} fusion(bf16[4096,1024]{1,0:T(8,128)(2,1)} %all-gather.11.cloned.1.call-done, f32[4096]{0:T(1024)S(1)} %convert_element_type.80, f32[128]{0:T(128)S(1)} %add_rsqrt_fusion, f32[128]{0:T(128)S(1)} %broadcast_multiply_fusion.1, bf16[128,8192]{1,0:T(8,128)(2,1)S(1)} %constant_dynamic-update-slice_fusion, ...), kind=kOutput, calls=%fused_computation.27 | convolution fusion | flops 1076363264 | bytes 9978884 | tf_op jit(solution)/shard_map/dot_general | solution.py:117
  340.8 2.1 convolution_convert_fusion.1
  343.3 0.9 copy.46
  (85 shorter events, 9.4 us)
Async XLA Ops:
  8.0 33.1 %all-gather.5.cloned.1.call-start = ((), (), s32[]{:S(2)}) async-start(), calls=%async_computation.3 | async-start | bytes 1310720 | tf_op jit(solution)/shard_map/all_gather | solution.py:81
  8.7 263.5 %reduce-scatter.2.cloned.1.call-start = ((), (), s32[]{:S(2)}) async-start(), calls=%async_computation.4 | async-start | bytes 10485760 | tf_op jit(solution)/shard_map/reduce_scatter | solution.py:99
  41.1 3.2 copy-start
  101.1 1.9 copy-start.1
  129.0 203.4 %all-gather.9.cloned.1.call-start = ((), (), s32[]{:S(2)}) async-start(), calls=%async_computation.6 | async-start | bytes 2621440 | tf_op jit(solution)/shard_map/all_gather | solution.py:124
  129.5 205.0 %all-gather.11.cloned.1.call-start = ((), (), s32[]{:S(2)}) async-start(), calls=%async_computation.7 | async-start | bytes 10485760 | tf_op jit(solution)/shard_map/all_gather | solution.py:119
  272.2 4.0 %copy-start.5 = (s32[128,2]{0,1:T(2,128)S(1)}, s32[128,2]{0,1:T(2,128)}, u32[]{:S(2)}) copy-start(s32[128,2]{0,1:T(2,128)} %param.15) | copy-start | bytes 3076
  272.2 29.4 %all-to-all-start.1 = ((f32[4,128,1024]{2,1,0:T(8,128)}), f32[4,128,1024]{2,1,0:T(8,128)S(1)}, u32[]{:S(2)}, u32[]{:S(2)}) async-start(f32[4,128,1024]{2,1,0:T(8,128)} %bitcast.91), calls=%async_computation.2 | async-start | bytes 4194304 | tf_op jit(solution)/shard_map/all_to_all | solution.py:100
  275.9 64.8 %all-gather.7.cloned.1.call-start = ((), (), s32[]{:S(2)}) async-start(), calls=%async_computation.5 | async-start | bytes 2621440 | tf_op jit(solution)/shard_map/all_gather | solution.py:129
  302.7 2.0 copy-start.3
  303.3 2.7 copy-start.6
  303.3 19.9 %copy-start.4 = (bf16[4096]{0:T(1024)(128)(2,1)S(1)}, bf16[4096]{0:T(1024)(128)(2,1)}, u32[]{:S(2)}) copy-start(bf16[4096]{0:T(1024)(128)(2,1)} %param.20) | copy-start | bytes 24580
  304.8 26.8 %copy-start.2 = (bf16[128,1024]{1,0:T(8,128)(2,1)}, bf16[128,1024]{1,0:T(8,128)(2,1)S(1)}, u32[]{:S(2)}) copy-start(bf16[128,1024]{1,0:T(8,128)(2,1)S(1)} %add_convert_fusion.1) | copy-start | bytes 786436
  304.8 9.7 %collective-permute-start = (bf16[128,1024]{1,0:T(8,128)(2,1)S(1)}, bf16[128,1024]{1,0:T(8,128)(2,1)S(1)}, u32[]{:S(2)}, u32[]{:S(2)}) collective-permute-start(bf16[128,1024]{1,0:T(8,128)(2,1)S(1)} %add_convert_fusion.1), channel_id=1, source_target_pairs={{0,1},{1,2},{2,3},{3,0},{4,5},{5,6},{6,7},{7,4},{8,9},{9,10},{10,1... | collective-permute-start | bytes 786440 | tf_op jit(solution)/shard_map/ppermute | solution.py:112
  314.5 8.7 %collective-permute-start.1 = (bf16[128,1024]{1,0:T(8,128)(2,1)S(1)}, bf16[128,1024]{1,0:T(8,128)(2,1)S(1)}, u32[]{:S(2)}, u32[]{:S(2)}) collective-permute-start(bf16[128,1024]{1,0:T(8,128)(2,1)S(1)} %collective-permute-done), channel_id=1, source_target_pairs={{0,1},{1,2},{2,3},{3,0},{4,5},{5,6},{6,7},{7,4},{8,9},{9,10},{10,1... | collective-permute-start | bytes 786440 | tf_op jit(solution)/shard_map/ppermute | solution.py:112
  323.2 8.2 %collective-permute-start.2 = (bf16[128,1024]{1,0:T(8,128)(2,1)S(1)}, bf16[128,1024]{1,0:T(8,128)(2,1)S(1)}, u32[]{:S(2)}, u32[]{:S(2)}) collective-permute-start(bf16[128,1024]{1,0:T(8,128)(2,1)S(1)} %collective-permute-done.1), channel_id=1, source_target_pairs={{0,1},{1,2},{2,3},{3,0},{4,5},{5,6},{6,7},{7,4},{8,9},{9,10},{10,1... | collective-permute-start | bytes 786440 | tf_op jit(solution)/shard_map/ppermute | solution.py:112
Sparse Core Ops, SparseCore 0:
  10.4 30.6 all-gather.4
  129.1 143.0 reduce-scatter.1
Sparse Core Ops, SparseCore 1:
  131.0 21.0 all-gather.8
  153.5 58.1 all-gather.10
  306.1 21.7 all-gather.6
